TPU v7x, 32 devices: a whole 2x2x4 slice. The times are simulated.
32 devices in a mesh: dp: 8 (over y, x, core), mp: 4 (over z).
Axes of the slice: x: 2, y: 2, z: 4, core: 2. Of those that a mesh axis runs over, the one named last changes fastest.
Arguments:
- pre: bfloat16 [1024, 12288], P('dp', 'mp'), may hold values from -32 to 32
- weight: float32 [6144, 12288], P('dp', 'mp'), may hold values from -0.0546875 to 0.0546875
- target: bfloat16 [6144, 1024], P('dp'), may hold values from -100 to 100
Outputs:
- update: float32 [6144, 12288], P('dp', 'mp')
All inputs are finite; a program needn't handle non-finite values.
Results may differ from a plain program's by a relative error of at most 0.0003.
The roundings to bfloat16 on the way count: a program that leaves them out, or rounds other values in their place, can miss the bound.
Values may be sent and summed in bfloat16 or wider, within the bound.
A program may use at most 64 MiB of HBM per device.

v0:
```python
import jax
import jax.numpy as jnp
from jax import lax
from jax.sharding import PartitionSpec as P

radius = 0.005
epsilon = 1e-06


def on_device(pre, weight, target):
    hidden = jax.nn.gelu(pre.astype(jnp.float32), approximate=False).astype(jnp.bfloat16)
    everyone = lax.all_gather(hidden, "dp", axis=0, tiled=True)
    entries = weight.shape[0] * weight.shape[1] * lax.axis_size("dp") * lax.axis_size("mp")

    def residual_of(matrix):
        partial_out = lax.dot_general(
            matrix, everyone, (((1,), (1,)), ((), ())), preferred_element_type=jnp.float32
        )
        summed = lax.psum(partial_out, "mp")
        result = (summed - target.astype(jnp.float32)).astype(jnp.bfloat16)
        return result

    resid = residual_of(weight.astype(jnp.bfloat16))
    ascent = jnp.dot(resid, everyone, preferred_element_type=jnp.float32)
    ascent_ms = lax.psum(jnp.sum(ascent * ascent), ("dp", "mp")) / entries
    perturbed = (weight + radius * jnp.tanh(ascent / jnp.sqrt(ascent_ms + epsilon))).astype(
        jnp.bfloat16
    )
    resid_two = residual_of(perturbed)
    descent = jnp.dot(resid_two, everyone, preferred_element_type=jnp.float32)
    descent_ms = lax.psum(jnp.sum(descent * descent), ("dp", "mp")) / entries
    return descent / jnp.sqrt(descent_ms + epsilon)


def solution(mesh):
    return jax.shard_map(
        on_device,
        mesh=mesh,
        in_specs=(P("dp", "mp"), P("dp", "mp"), P("dp", None)),
        out_specs=P("dp", "mp"),
        check_vma=False,
    )
```

profile of v0, /device:TPU:0, one launch (start us, length us, event | category | flops | bytes accessed | tf_op | source)
XLA Modules:
  0.0 443.9 jit_solution(3158897468256516652)
XLA Ops:
  6.5 0.0 all-gather.2.cloned.1.call-start
  6.5 5.1 %fusion.9 = bf16[128,3072]{1,0:T(8,128)(2,1)} fusion(bf16[128,3072]{1,0:T(8,128)(2,1)} %param.3), kind=kLoop, calls=%fused_computation.16 | loop fusion | flops 25952256 | bytes 1572864 | tf_op jit(solution)/shard_map/convert_element_type | solution.py:11
  11.7 0.0 all-gather.2.cloned.1.call-update
  11.7 0.0 all-reduce.3.cloned.1.call-start
  11.8 48.3 %all-gather.2.cloned.1.call-done = bf16[1024,3072]{1,0:T(8,128)(2,1)} async-done(((bf16[128,3072]{1,0:T(8,128)(2,1)}), bf16[1024,3072]{1,0:T(8,128)(2,1)}) %all-gather.2.cloned.1.call-update) | async-done | bytes 6291472 | tf_op jit(solution)/shard_map/all_gather | solution.py:12
  60.1 11.1 %fusion.5 = f32[768,1024]{1,0:T(8,128)} fusion(bf16[1024,3072]{1,0:T(8,128)(2,1)} %all-gather.2.cloned.1.call-done, f32[768,3072]{1,0:T(8,128)} %param.4), kind=kOutput, calls=%fused_computation.14 | convolution fusion | flops 4834197504 | bytes 18874368 | tf_op jit(solution)/shard_map/dot_general | solution.py:16
  71.2 0.0 copy-start
  71.2 0.0 all-reduce.3.cloned.1.call-update
  71.2 0.0 all-reduce.5.cloned.1.call-start
  71.2 121.2 %all-reduce.3.cloned.1.call-done = f32[768,1024]{1,0:T(8,128)} async-done(((f32[768,1024]{1,0:T(8,128)}), f32[768,1024]{1,0:T(8,128)}) %all-reduce.3.cloned.1.call-update) | async-done | bytes 3145744 | tf_op jit(solution)/shard_map/psum | solution.py:19
  192.4 0.0 copy-done
  192.4 11.1 %multiply_reduce_fusion.1 = (f32[]{:T(128)}, f32[768,3072]{1,0:T(8,128)}) fusion(bf16[1024,3072]{1,0:T(8,128)(2,1)} %all-gather.2.cloned.1.call-done, f32[768,1024]{1,0:T(8,128)} %all-reduce.3.cloned.1.call-done, bf16[768,1024]{1,0:T(8,128)(2,1)S(1)} %copy-done), kind=kOutput, calls=%fused_computation.2 | convolution fusion | flops 4838916096 | bytes 20447236 | tf_op jit(solution)/shard_map/dot_general | solution.py:24
  203.5 39.6 %psum.29 = f32[]{:T(128)} all-reduce(f32[]{:T(128)} %get-tuple-element.5), channel_id=1, replica_groups=mesh['dp'=8,'mp'=4] {'dp','mp'}, use_global_device_ids=true, to_apply=%region_2.0 | all-reduce | flops 1 | bytes 8 | tf_op jit(solution)/shard_map/psum | solution.py:25
  243.7 12.1 %fusion.2 = f32[768,1024]{1,0:T(8,128)} fusion(bf16[1024,3072]{1,0:T(8,128)(2,1)} %all-gather.2.cloned.1.call-done, f32[768,3072]{1,0:T(8,128)} %param.4, f32[768,3072]{1,0:T(8,128)} %get-tuple-element.6, f32[]{:T(128)S(6)} %sqrt.6), kind=kOutput, calls=%fused_computation.6 | convolution fusion | flops 4841275392 | bytes 28311556 | tf_op jit(solution)/shard_map/dot_general | solution.py:16
  255.8 0.0 all-reduce.5.cloned.1.call-update
  255.9 121.2 %all-reduce.5.cloned.1.call-done = f32[768,1024]{1,0:T(8,128)} async-done(((f32[768,1024]{1,0:T(8,128)}), f32[768,1024]{1,0:T(8,128)}) %all-reduce.5.cloned.1.call-update) | async-done | bytes 3145744 | tf_op jit(solution)/shard_map/psum | solution.py:19
  377.1 11.1 %multiply_reduce_fusion = (f32[]{:T(128)}, f32[768,3072]{1,0:T(8,128)}) fusion(bf16[1024,3072]{1,0:T(8,128)(2,1)} %all-gather.2.cloned.1.call-done, f32[768,1024]{1,0:T(8,128)} %all-reduce.5.cloned.1.call-done, bf16[768,1024]{1,0:T(8,128)(2,1)S(1)} %copy-done), kind=kOutput, calls=%fused_computation | convolution fusion | flops 4838916096 | bytes 20447236 | tf_op jit(solution)/shard_map/dot_general | solution.py:30
  388.2 39.4 %psum.31 = f32[]{:T(128)} all-reduce(f32[]{:T(128)} %get-tuple-element.7), channel_id=1, replica_groups=mesh['dp'=8,'mp'=4] {'dp','mp'}, use_global_device_ids=true, to_apply=%region_5.0 | all-reduce | flops 1 | bytes 8 | tf_op jit(solution)/shard_map/psum | solution.py:31
  428.3 9.0 %broadcast_divide_fusion = f32[768,3072]{1,0:T(8,128)} fusion(f32[768,3072]{1,0:T(8,128)} %get-tuple-element.8, f32[]{:T(128)S(6)} %sqrt.7), kind=kLoop, calls=%fused_computation.3 | loop fusion | flops 2359296 | bytes 18874372 | tf_op jit(solution)/shard_map/div | solution.py:32
Async XLA Ops:
  6.5 53.5 %all-gather.2.cloned.1.call-start = ((), (), s32[]{:S(2)}) async-start(), calls=%async_computation | async-start | bytes 7077888 | tf_op jit(solution)/shard_map/all_gather | solution.py:12
  11.7 180.7 %all-reduce.3.cloned.1.call-start = ((), (), s32[]{:S(2)}) async-start(), calls=%async_computation.1 | async-start | bytes 6291456 | tf_op jit(solution)/shard_map/psum | solution.py:19
  71.2 121.3 %copy-start = (bf16[768,1024]{1,0:T(8,128)(2,1)S(1)}, bf16[768,1024]{1,0:T(8,128)(2,1)}, u32[]{:S(2)}) copy-start(bf16[768,1024]{1,0:T(8,128)(2,1)} %param.5) | copy-start | bytes 4718596
  71.2 305.9 %all-reduce.5.cloned.1.call-start = ((), (), s32[]{:S(2)}) async-start(), calls=%async_computation.2 | async-start | bytes 6291456 | tf_op jit(solution)/shard_map/psum | solution.py:19
Sparse Core Ops, SparseCore 0:
  11.8 48.2 all-gather.1
  71.3 121.0 all-reduce.2
  256.0 121.0 all-reduce.4
where the time goes:
time: 444 us
  waiting for transfers between devices  291 us (66%)
  blocking collectives  79 us (18%)
  matrix products  45.4 us (10%)
  between operations  14.5 us (3%)
  other arithmetic  14.2 us (3%)
    psum x2, waiting for transfers between devices, residual_of(): summed = lax.psum(partial_out, 'mp')  242 us
    all_gather x1, waiting for transfers between devices, on_device(): everyone = lax.all_gather(hidden, 'dp', axis=0, tiled=True)  48.3 us
    psum x1, blocking collectives, on_device(): ascent_ms = lax.psum(jnp.sum(ascent * ascent), ('dp', 'mp')) / entries  39.6 us
    psum x1, blocking collectives, on_device(): descent_ms = lax.psum(jnp.sum(descent * descent), ('dp', 'mp')) / entries  39.4 us
    dot_general x2, matrix products, residual_of(): lax.dot_general(matrix, everyone, (((1,), (1,)), ((), ())), preferred_ele...  23.2 us
    dot_general x1, matrix products, on_device(): ascent = jnp.dot(resid, everyone, preferred_element_type=jnp.float32)  11.1 us
    dot_general x1, matrix products, on_device(): descent = jnp.dot(resid_two, everyone, preferred_element_type=jnp.float32)  11.1 us
    div x1, other arithmetic, on_device(): return descent / jnp.sqrt(descent_ms + epsilon)  9.05 us
  transfers between devices with their start and end apart: 3, of which 3 were waited for; matrix products, arithmetic and copies ran while one was open for 0% of the time, Pallas kernels for 0%

commit v1 on v0

--- a/solution.py
+++ b/solution.py
@@ -16,7 +16,8 @@
         partial_out = lax.dot_general(
             matrix, everyone, (((1,), (1,)), ((), ())), preferred_element_type=jnp.float32
         )
-        summed = lax.psum(partial_out, "mp")
+        shards = lax.all_gather(partial_out, "mp")
+        summed = jnp.sum(shards, axis=0)
         result = (summed - target.astype(jnp.float32)).astype(jnp.bfloat16)
         return result
 

time: 444 us -> 685 us (1.54)
  waiting for transfers between devices: 291 us -> 483 us
  other arithmetic: 14.2 us -> 41.9 us
  local copies, waits for them, and re-layouts: 0.01 us -> 21.4 us
    all_gather x0 -> x2, waiting for transfers between devices: none -> 435 us  [residual_of(): shards = lax.all_gather(partial_out, 'mp')]
    psum x2 -> x0, waiting for transfers between devices: 242 us -> none  [residual_of(): summed = lax.psum(partial_out, 'mp')]
    reduce_sum x0 -> x2, other arithmetic: none -> 27.7 us  [residual_of(): summed = jnp.sum(shards, axis=0)]
    all_gather x0 -> x1, local copies, waits for them, and re-layouts: none -> 15.8 us  [residual_of(): shards = lax.all_gather(partial_out, 'mp')]
where the time goes in v1:
time: 685 us
  waiting for transfers between devices  483 us (71%)
  blocking collectives  77.3 us (11%)
  matrix products  46.2 us (7%)
  other arithmetic  41.9 us (6%)
  local copies, waits for them, and re-layouts  21.4 us (3%)
  between operations  14.5 us (2%)
    all_gather x2, waiting for transfers between devices, residual_of(): shards = lax.all_gather(partial_out, 'mp')  435 us
    all_gather x1, waiting for transfers between devices, on_device(): everyone = lax.all_gather(hidden, 'dp', axis=0, tiled=True)  48.3 us
    psum x1, blocking collectives, on_device(): ascent_ms = lax.psum(jnp.sum(ascent * ascent), ('dp', 'mp')) / entries  38.8 us
    psum x1, blocking collectives, on_device(): descent_ms = lax.psum(jnp.sum(descent * descent), ('dp', 'mp')) / entries  38.5 us
    reduce_sum x2, other arithmetic, residual_of(): summed = jnp.sum(shards, axis=0)  27.7 us
    dot_general x2, matrix products, residual_of(): lax.dot_general(matrix, everyone, (((1,), (1,)), ((), ())), preferred_ele...  23.1 us
    all_gather x1, local copies, waits for them, and re-layouts, residual_of(): shards = lax.all_gather(partial_out, 'mp')  15.8 us
  transfers between devices with their start and end apart: 3, of which 3 were waited for; matrix products, arithmetic and copies ran while one was open for 0% of the time, Pallas kernels for 0%

profile of v1, /device:TPU:0, one launch (start us, length us, event | category | flops | bytes accessed | tf_op | source)
XLA Modules:
  0.0 684.5 jit_solution(12425069250434969560)
XLA Ops:
  6.5 0.0 all-gather.6.cloned.1.call-start
  6.5 5.1 fusion.9
  11.7 0.0 all-gather.6.cloned.1.call-update
  11.7 0.0 all-gather.8.cloned.1.call-start
  11.8 48.3 %all-gather.6.cloned.1.call-done = bf16[1024,3072]{1,0:T(8,128)(2,1)} async-done(((bf16[128,3072]{1,0:T(8,128)(2,1)}), bf16[1024,3072]{1,0:T(8,128)(2,1)}) %all-gather.6.cloned.1.call-update) | async-done | bytes 6291472 | tf_op jit(solution)/shard_map/all_gather | solution.py:12
  60.1 11.1 %fusion.5 = f32[768,1024]{0,1:T(8,128)} fusion(bf16[1024,3072]{1,0:T(8,128)(2,1)} %all-gather.6.cloned.1.call-done, f32[768,3072]{1,0:T(8,128)} %param.4), kind=kOutput, calls=%fused_computation.14 | convolution fusion | flops 4834197504 | bytes 18874368 | tf_op jit(solution)/shard_map/dot_general | solution.py:16
  71.2 0.0 copy-start
  71.2 0.0 all-gather.8.cloned.1.call-update
  71.2 0.0 all-gather.10.cloned.1.call-start
  71.2 1.3 copy-done
  72.6 0.7 copy.5
  73.3 216.3 %all-gather.8.cloned.1.call-done = f32[3072,1024]{0,1:T(8,128)} async-done(((f32[768,1024]{0,1:T(8,128)}), f32[3072,1024]{0,1:T(8,128)}) %all-gather.8.cloned.1.call-update) | async-done | bytes 12582928 | tf_op jit(solution)/shard_map/all_gather | solution.py:19
  289.6 15.8 %reshape = f32[4,768,1024]{1,0,2:T(4,128)} reshape(f32[3072,1024]{0,1:T(8,128)} %all-gather.8.cloned.1.call-done) | data formatting | bytes 25165824 | tf_op jit(solution)/shard_map/all_gather | solution.py:19
  305.3 19.6 %reduce_sum.36 = f32[768,1024]{0,1:T(8,128)} reduce(f32[4,768,1024]{1,0,2:T(4,128)} %reshape, f32[]{:T(128)} %constant.11.clone.1), dimensions={0}, to_apply=%region_0.0 | reduce | flops 2359296 | bytes 15728644 | tf_op jit(solution)/shard_map/reduce_sum | solution.py:20
  324.9 11.6 %multiply_reduce_fusion.1 = (f32[]{:T(128)}, f32[768,3072]{1,0:T(8,128)}) fusion(bf16[1024,3072]{1,0:T(8,128)(2,1)} %all-gather.6.cloned.1.call-done, f32[768,1024]{0,1:T(8,128)} %reduce_sum.36, bf16[768,1024]{0,1:T(8,128)(2,1)S(1)} %copy.5), kind=kOutput, calls=%fused_computation.2 | convolution fusion | flops 4838916096 | bytes 20447236 | tf_op jit(solution)/shard_map/dot_general | solution.py:25
  336.5 38.8 %psum.14 = f32[]{:T(128)} all-reduce(f32[]{:T(128)} %get-tuple-element.5), channel_id=1, replica_groups=mesh['dp'=8,'mp'=4] {'dp','mp'}, use_global_device_ids=true, to_apply=%region_2.0 | all-reduce | flops 1 | bytes 8 | tf_op jit(solution)/shard_map/psum | solution.py:26
  376.0 12.0 %fusion.2 = f32[768,1024]{1,0:T(8,128)} fusion(bf16[1024,3072]{1,0:T(8,128)(2,1)} %all-gather.6.cloned.1.call-done, f32[768,3072]{1,0:T(8,128)} %param.4, f32[768,3072]{1,0:T(8,128)} %get-tuple-element.6, f32[]{:T(128)S(6)} %sqrt.6), kind=kOutput, calls=%fused_computation.6 | convolution fusion | flops 4841275392 | bytes 28311556 | tf_op jit(solution)/shard_map/dot_general | solution.py:16
  388.0 0.0 all-gather.10.cloned.1.call-update
  388.0 218.4 %all-gather.10.cloned.1.call-done = f32[3072,1024]{1,0:T(8,128)} async-done(((f32[768,1024]{1,0:T(8,128)}), f32[3072,1024]{1,0:T(8,128)}) %all-gather.10.cloned.1.call-update) | async-done | bytes 12582928 | tf_op jit(solution)/shard_map/all_gather | solution.py:19
  606.5 8.1 %reduce_sum.38 = f32[768,1024]{1,0:T(8,128)} reduce(f32[4,768,1024]{2,1,0:T(8,128)} %bitcast.9, f32[]{:T(128)} %constant.11.clone.1), dimensions={0}, to_apply=%region_3.0 | reduce | flops 2359296 | bytes 15728644 | tf_op jit(solution)/shard_map/reduce_sum | solution.py:20
  614.6 3.5 copy.6
  618.1 11.5 %multiply_reduce_fusion = (f32[]{:T(128)}, f32[768,3072]{1,0:T(8,128)}) fusion(bf16[1024,3072]{1,0:T(8,128)(2,1)} %all-gather.6.cloned.1.call-done, f32[768,1024]{0,1:T(8,128)} %copy.6, bf16[768,1024]{0,1:T(8,128)(2,1)S(1)} %copy.5), kind=kOutput, calls=%fused_computation | convolution fusion | flops 4838916096 | bytes 20447236 | tf_op jit(solution)/shard_map/dot_general | solution.py:31
  629.7 38.5 %psum.15 = f32[]{:T(128)} all-reduce(f32[]{:T(128)} %get-tuple-element.7), channel_id=1, replica_groups=mesh['dp'=8,'mp'=4] {'dp','mp'}, use_global_device_ids=true, to_apply=%region_5.0 | all-reduce | flops 1 | bytes 8 | tf_op jit(solution)/shard_map/psum | solution.py:32
  668.9 9.0 %broadcast_divide_fusion = f32[768,3072]{1,0:T(8,128)} fusion(f32[768,3072]{1,0:T(8,128)} %get-tuple-element.8, f32[]{:T(128)S(6)} %sqrt.7), kind=kLoop, calls=%fused_computation.3 | loop fusion | flops 2359296 | bytes 18874372 | tf_op jit(solution)/shard_map/div | solution.py:33
Async XLA Ops:
  6.5 53.5 %all-gather.6.cloned.1.call-start = ((), (), s32[]{:S(2)}) async-start(), calls=%async_computation | async-start | bytes 7077888 | tf_op jit(solution)/shard_map/all_gather | solution.py:12
  11.7 277.8 %all-gather.8.cloned.1.call-start = ((), (), s32[]{:S(2)}) async-start(), calls=%async_computation.1 | async-start | bytes 15728640 | tf_op jit(solution)/shard_map/all_gather | solution.py:19
  71.2 1.4 copy-start
  71.2 535.3 %all-gather.10.cloned.1.call-start = ((), (), s32[]{:S(2)}) async-start(), calls=%async_computation.2 | async-start | bytes 15728640 | tf_op jit(solution)/shard_map/all_gather | solution.py:19
Sparse Core Ops, SparseCore 0:
  11.8 48.2 all-gather.5
  71.3 218.1 all-gather.7
  388.2 218.2 all-gather.9
